TPU v7x, 32 devices: a whole 2x2x4 slice. The times are simulated.
32 devices in a mesh: tm: 4 (over z), space: 8 (over y, x, core).
Axes of the slice: x: 2, y: 2, z: 4, core: 2. Of those that a mesh axis runs over, the one named last changes fastest.
Arguments:
- frames: bfloat16 [4, 96, 32, 1280], P('tm', None, 'space'), may hold values from -6 to 6
- cache: bfloat16 [2, 96, 32, 1280], P(None, 'tm', 'space'), may hold values from -6 to 6
- grad_out: bfloat16 [4, 96, 32, 1280], P('tm', None, 'space'), may hold values from -6 to 6
- weight: bfloat16 [3, 3, 3, 96, 96], replicated, may hold values from -0.125 to 0.125
Outputs:
- input_grad: bfloat16 [4, 96, 32, 1280], P('tm', None, 'space')
- cache_grad: bfloat16 [2, 96, 32, 1280], P(None, 'tm', 'space')
- weight_grad: float32 [3, 3, 3, 96, 96], replicated
All inputs are finite; a program needn't handle non-finite values.
Results may differ from a plain program's by a relative error of at most 0.0041.
Values may be sent and summed in bfloat16 or wider, within the bound.
A program may use at most 64 MiB of HBM per device.

v0:
```python
import functools
import math

import jax
import jax.numpy as jnp
from jax import lax
from jax.experimental import pallas as pl
from jax.experimental.pallas import tpu as pltpu
from jax.sharding import PartitionSpec as P

MESH = pl.DeviceIdType.MESH
OWN, N1, N2, C1, C0 = range(5)
TO_PREV, FWD_PREV, TO_NEXT, FWD_C1, FWD_C0 = range(5)


def kernel(
    nz, ns, ck, channels, share,
    g_ref, x_ref, c_ref, wt_ref, wc_ref, ig_ref, cg_ref, wg_ref,
    gp, sc, dacc, wtmp, acc, xs_ref, wl_ref,
    sb, rb, zs, zb, gb,
    z_send, z_recv, h_send, h_recv,
    rs_send, rs_recv, zz_send, zz_recv, ag_send, ag_recv,
):
    assert nz == 4
    j = lax.axis_index("tm")
    s = lax.axis_index("space")
    rows, _, cols = g_ref.shape
    k_row = 3 * channels
    taps = 3 * k_row
    last = nz - 1
    order = [0, rows - 1, *range(1, rows - 1)]
    high = 128
    late = jnp.where(j < last - 1, N2, C1)

    barrier = pltpu.get_barrier_semaphore()
    for k in range(1, ns):
        pl.semaphore_signal(barrier, inc=1, device_id={"space": lax.rem(s + k, ns)}, device_id_type=MESH)
    for k in range(1, nz):
        pl.semaphore_signal(barrier, inc=1, device_id={"tm": lax.rem(j + k, nz)}, device_id_type=MESH)
    pl.semaphore_wait(barrier, ns - 1 + nz - 1)

    def row_copy(stream, slot_from, slot_to, r, target):
        src = g_ref.at[r] if slot_from == OWN else gp.at[slot_from, r + 1]
        return pltpu.make_async_remote_copy(
            src_ref=src, dst_ref=gp.at[slot_to, r + 1],
            send_sem=z_send.at[stream, r], recv_sem=z_recv.at[slot_to, r],
            device_id={"tm": target}, device_id_type=MESH)

    prev = lax.rem(j + nz - 1, nz)
    nxt = lax.rem(j + 1, nz)

    def to_prev(r):
        return row_copy(TO_PREV, OWN, N1, r, prev)

    def fwd_prev(r):
        return row_copy(FWD_PREV, N1, N2, r, prev)

    def own_c0(r):
        return row_copy(TO_NEXT, OWN, C0, r, nxt)

    def own_c1(r):
        return row_copy(TO_NEXT, OWN, C1, r, nxt)

    def fwd_c1(r):
        return row_copy(FWD_C1, C1, C1, r, nxt)

    def fwd_c0(r):
        return row_copy(FWD_C0, C0, C0, r, nxt)

    for r in order:
        pl.when(j >= 1)(lambda: to_prev(r).start())
        pl.when(j == 0)(lambda: own_c0(r).start())
    pl.when(j == 1)(lambda: own_c1(order[0]).start())

    def halo_up(slot):
        src = g_ref.at[0] if slot is OWN else gp.at[slot, 1]
        return pltpu.make_async_remote_copy(
            src_ref=src, dst_ref=gp.at[slot, rows + 1],
            send_sem=h_send.at[slot, 0], recv_sem=h_recv.at[slot, 0],
            device_id={"space": lax.rem(s + ns - 1, ns)}, device_id_type=MESH)

    def halo_down(slot):
        src = g_ref.at[rows - 1] if slot is OWN else gp.at[slot, rows]
        return pltpu.make_async_remote_copy(
            src_ref=src, dst_ref=gp.at[slot, 0],
            send_sem=h_send.at[slot, 1], recv_sem=h_recv.at[slot, 1],
            device_id={"space": lax.rem(s + 1, ns)}, device_id_type=MESH)

    def halo_start_up(slot):
        pl.when(s >= 1)(lambda: halo_up(slot).start())

    def halo_start_down(slot):
        pl.when(s < ns - 1)(lambda: halo_down(slot).start())

    def halo_wait(slot):
        @pl.when(s >= 1)
        def _():
            halo_up(slot).wait_send()
            halo_down(slot).wait_recv()

        @pl.when(s < ns - 1)
        def _():
            halo_down(slot).wait_send()
            halo_up(slot).wait_recv()

    halo_start_up(OWN)
    halo_start_down(OWN)

    @pl.when(s == 0)
    def _():
        for slot in range(5):
            gp[slot, 0] = jnp.zeros(gp.shape[2:], gp.dtype)

    @pl.when(s == ns - 1)
    def _():
        for slot in range(5):
            gp[slot, rows + 1] = jnp.zeros(gp.shape[2:], gp.dtype)

    for r in range(rows):
        gp[OWN, r + 1] = g_ref[r]
    wtmp[...] = jnp.zeros_like(wtmp)
    acc[...] = jnp.zeros_like(acc)
    stack = xs_ref.shape[1]
    xs_ref[:, channels:, :] = jnp.zeros((rows, stack - channels, cols), xs_ref.dtype)
    wl_ref[:, channels:, :] = jnp.zeros((5, stack - channels, taps), wl_ref.dtype)
    for h in range(rows):
        xs_ref[h, :channels, :] = x_ref[h]
        xs_ref[h, channels:channels + share, :] = c_ref[0, h]
        xs_ref[h, high:high + share, :] = c_ref[1, h]
    for slot, tap in ((OWN, 2), (N1, 1), (N2, 0)):
        wl_ref[slot, :channels, :] = wt_ref[tap]
    for slot in (C1, C0):
        wl_ref[slot, :channels, :] = jnp.zeros((channels, taps), wl_ref.dtype)

    def weights_g0(slot):
        wl_ref[slot, channels:channels + share, :] = wc_ref[0]
        wl_ref[slot, high:high + share, :] = wc_ref[1]

    def weights_g1(slot):
        wl_ref[slot, high:high + share, :] = wc_ref[0]

    @pl.when(j == 0)
    def _():
        weights_g0(OWN)
        weights_g1(N1)

    pl.when(j == 1)(lambda: weights_g1(OWN))
    weights_g1(C1)
    weights_g0(C0)

    lane = lax.broadcasted_iota(jnp.int32, (channels, cols), 1)
    wide = 128
    wlane = lax.broadcasted_iota(jnp.int32, (taps, wide), 1)

    def shift_row(slot, p):
        value = gp[slot, p]
        full = value.astype(jnp.float32)
        ahead = jnp.where(lane == cols - 1, 0.0, pltpu.roll(full, cols - 1, 1))
        behind = jnp.where(lane == 0, 0.0, pltpu.roll(full, 1, 1))
        base = pl.multiple_of(p * k_row, 16)
        sc[pl.ds(base, channels), :] = ahead.astype(jnp.bfloat16)
        sc[pl.ds(pl.multiple_of(base + channels, 16), channels), :] = value
        sc[pl.ds(pl.multiple_of(base + 2 * channels, 16), channels), :] = behind.astype(jnp.bfloat16)

    def compute_row(slot, h):
        block = sc[pl.ds(pl.multiple_of(h * k_row, 16), taps), :]
        term = jnp.dot(wl_ref[slot], block, preferred_element_type=jnp.float32)
        if slot is OWN:
            dacc[h] = term
        else:
            dacc[h] += term
        wtmp[:, :stack] += lax.dot_general(
            block, xs_ref[h], (((1,), (1,)), ((), ())), preferred_element_type=jnp.float32)

    def placed_cache(block, shift_from):
        turned = pltpu.roll(block, lax.rem(j * share + 2 * wide - shift_from, wide), 1)
        inside = jnp.logical_and(wlane >= j * share, wlane < (j + 1) * share)
        return jnp.where(inside, turned, 0.0)

    def run(step, start, stop):
        def body(i, carry):
            step(i)
            return carry

        lax.fori_loop(start, stop, body, 0)

    def process(slot):
        run(functools.partial(shift_row, slot), 0, rows + 2)
        run(functools.partial(compute_row, slot), 0, rows)

    def add_x(tap):
        acc[tap, :taps, :] += jnp.where(wlane < channels, wtmp[:, :wide], 0.0)

    def add_g0():
        acc[0, :taps, :] += placed_cache(wtmp[:, :wide], channels)
        acc[1, :taps, :] += placed_cache(wtmp[:, wide:], 0)

    def add_g1():
        acc[0, :taps, :] += placed_cache(wtmp[:, wide:], 0)

    def clear():
        wtmp[...] = jnp.zeros_like(wtmp)

    def reduction(index):
        def rs_copy(k):
            to = lax.rem(s + k, ns)
            return pltpu.make_async_remote_copy(
                src_ref=sb.at[index, to], dst_ref=rb.at[index, s],
                send_sem=rs_send.at[index, k], recv_sem=rs_recv.at[index, s],
                device_id={"space": to}, device_id_type=MESH)

        def rs_landed(k):
            source = lax.rem(s + ns - k, ns)
            return pltpu.make_async_remote_copy(
                src_ref=sb.at[index, source], dst_ref=rb.at[index, source],
                send_sem=rs_send.at[index, k], recv_sem=rs_recv.at[index, source],
                device_id={"space": source}, device_id_type=MESH)

        def z_copy(k):
            return pltpu.make_async_remote_copy(
                src_ref=zs.at[index], dst_ref=zb.at[index, j],
                send_sem=zz_send.at[index, k], recv_sem=zz_recv.at[index, j],
                device_id={"tm": lax.rem(j + k, nz)}, device_id_type=MESH)

        def z_landed(k):
            source = lax.rem(j + nz - k, nz)
            return pltpu.make_async_remote_copy(
                src_ref=zs.at[index], dst_ref=zb.at[index, source],
                send_sem=zz_send.at[index, k], recv_sem=zz_recv.at[index, source],
                device_id={"tm": source}, device_id_type=MESH)

        def ag_copy(k):
            return pltpu.make_async_remote_copy(
                src_ref=gb.at[index, s], dst_ref=gb.at[index, s],
                send_sem=ag_send.at[index, k], recv_sem=ag_recv.at[index, s],
                device_id={"space": lax.rem(s + k, ns)}, device_id_type=MESH)

        def ag_landed(k):
            source = lax.rem(s + ns - k, ns)
            return pltpu.make_async_remote_copy(
                src_ref=gb.at[index, source], dst_ref=gb.at[index, source],
                send_sem=ag_send.at[index, k], recv_sem=ag_recv.at[index, source],
                device_id={"space": source}, device_id_type=MESH)

        def scatter():
            for q in range(ns):
                sb[index, q] = acc[index, q * ck:(q + 1) * ck, :].astype(jnp.bfloat16)
            for k in range(1, ns):
                rs_copy(k).start()

        def across():
            total = acc[index, pl.ds(pl.multiple_of(s * ck, 16), ck), :]
            for k in range(1, ns):
                rs_landed(k).wait_recv()
                total = total + rb[index, lax.rem(s + ns - k, ns)].astype(jnp.float32)
            zs[index] = total.astype(jnp.bfloat16)
            for k in range(1, nz):
                z_copy(k).start()

        def gather():
            zb[index, j] = zs[index]
            for k in range(1, nz):
                z_landed(k).wait_recv()
            total = zb[index, 0].astype(jnp.float32)
            for q in range(1, nz):
                total = total + zb[index, q].astype(jnp.float32)
            gb[index, s] = total.astype(jnp.bfloat16)
            for k in range(1, ns):
                ag_copy(k).start()

        def finish():
            for k in range(1, ns):
                ag_landed(k).wait_recv()
            for q in range(ns):
                acc[index, q * ck:(q + 1) * ck, :] = gb[index, q].astype(jnp.float32)
            for b in range(3):
                for d in range(3):
                    at = (b * 3 + d) * channels
                    wg_ref[index, 2 - b, d] = acc[index, at:at + channels, :channels]
            for k in range(1, ns):
                rs_copy(k).wait_send()
                ag_copy(k).wait_send()
            for k in range(1, nz):
                z_copy(k).wait_send()

        return scatter, across, gather, finish

    steps = [reduction(tap) for tap in range(3)]
    scatter, across, gather, finish = range(4)

    has_n1 = j < last
    passes_on = j < last

    def c1_row(r):
        @pl.when(j >= 2)
        def _():
            own_c1(r).wait_recv()
            pl.when(passes_on)(lambda: fwd_c1(r).start())

    def halo_after(slot, r):
        if r == 0:
            halo_start_up(slot)
        if r == rows - 1:
            halo_start_down(slot)

    def c0_row(r):
        own_c0(r).wait_recv()
        pl.when(passes_on)(lambda: fwd_c0(r).start())
        halo_after(C0, r)

    c1_row(order[0])
    pl.when(j == 1)(lambda: c0_row(order[0]))
    halo_wait(OWN)
    process(OWN)
    add_x(2)
    steps[2][scatter]()
    pl.when(j == 0)(add_g0)
    pl.when(j == 1)(add_g1)
    clear()

    for count, r in enumerate(order):
        pl.when(j >= (2 if count == 0 else 1))(lambda: c0_row(r))

        @pl.when(has_n1)
        def _():
            to_prev(r).wait_recv()
            pl.when(j >= 1)(lambda: fwd_prev(r).start())
            halo_after(N1, r)


    @pl.when(j == 1)
    def _():
        for r in order[1:]:
            own_c1(r).start()

    @pl.when(has_n1)
    def _():
        halo_wait(N1)
        process(N1)
        add_x(1)
        pl.when(j == 0)(add_g1)
        clear()

    c1_row(order[1])

    @pl.when(j >= 1)
    def _():
        halo_wait(C0)
        process(C0)
        add_g0()
        clear()

    steps[1][scatter]()
    for r in order[2:-1]:
        c1_row(r)

    def late_row(r):
        row_copy(FWD_PREV, N1, late, r, prev).wait_recv()

    for r in order[:-1]:
        @pl.when(j < last - 1)
        def _():
            late_row(r)

        halo_after(late, r)
    missing = order[-1] + 1
    halo_wait(late)
    run(functools.partial(shift_row, late), 0, missing)
    run(functools.partial(shift_row, late), missing + 1, rows + 2)
    run(functools.partial(compute_row, late), 0, missing - 2)
    c1_row(order[-1])
    steps[2][across]()
    steps[1][across]()

    @pl.when(j < last - 1)
    def _():
        late_row(order[-1])

    shift_row(late, missing)
    run(functools.partial(compute_row, late), missing - 2, rows)
    pl.when(j < last - 1)(lambda: add_x(0))
    pl.when(j >= last - 1)(add_g1)
    steps[0][scatter]()
    steps[2][gather]()
    steps[1][gather]()
    for h in range(rows):
        ig_ref[h] = dacc[h, :channels, :].astype(jnp.bfloat16)
        cg_ref[0, h] = dacc[h, channels:channels + share, :].astype(jnp.bfloat16)
        cg_ref[1, h] = dacc[h, high:high + share, :].astype(jnp.bfloat16)
    steps[0][across]()
    steps[2][finish]()
    steps[1][finish]()
    steps[0][gather]()

    for r in range(rows):
        @pl.when(j >= 1)
        def _():
            to_prev(r).wait_send()

        @pl.when(jnp.logical_and(j >= 1, has_n1))
        def _():
            fwd_prev(r).wait_send()

        @pl.when(j == 0)
        def _():
            own_c0(r).wait_send()

        @pl.when(j == 1)
        def _():
            own_c1(r).wait_send()

        @pl.when(jnp.logical_and(j >= 1, passes_on))
        def _():
            fwd_c0(r).wait_send()

        @pl.when(jnp.logical_and(j >= 2, passes_on))
        def _():
            fwd_c1(r).wait_send()
    steps[0][finish]()


def up_to(value, step):
    return -(-value // step) * step


def per_device(nz, ns, frames, cache, grad_out, weight):
    j = lax.axis_index("tm")
    _, channels, rows, cols = frames.shape
    share = cache.shape[1]
    taps = 9 * channels
    stack = 128 + up_to(share, 32)
    ck = up_to(-(-taps // ns), 16)
    g = jnp.transpose(grad_out[0], (1, 0, 2))
    x = jnp.transpose(frames[0], (1, 0, 2))
    c = jnp.transpose(cache, (0, 2, 1, 3))
    wt = jnp.transpose(weight[:, ::-1], (0, 4, 1, 2, 3)).reshape(3, channels, taps)
    wc = lax.dynamic_slice_in_dim(wt[:2], j * share, share, axis=1)
    scale = 1.0 / math.sqrt(nz * ns * rows * cols)
    f32, bf16 = jnp.float32, jnp.bfloat16
    vmem = pl.BlockSpec(memory_space=pltpu.VMEM)
    dma = pltpu.SemaphoreType.DMA
    ig, cg, weight_grad = pl.pallas_call(
        functools.partial(kernel, nz, ns, ck, channels, share),
        out_shape=(
            jax.ShapeDtypeStruct((rows, channels, cols), bf16),
            jax.ShapeDtypeStruct((2, rows, share, cols), bf16),
            jax.ShapeDtypeStruct(weight.shape, f32),
        ),
        in_specs=[vmem] * 5,
        out_specs=(vmem,) * 3,
        scratch_shapes=[
            pltpu.VMEM((5, rows + 2, channels, cols), bf16),
            pltpu.VMEM(((rows + 2) * 3 * channels, cols), bf16),
            pltpu.VMEM((rows, stack, cols), f32),
            pltpu.VMEM((taps, 256), f32),
            pltpu.VMEM((3, ns * ck, 128), f32),
            pltpu.VMEM((rows, stack, cols), bf16),
            pltpu.VMEM((5, stack, taps), bf16),
            pltpu.VMEM((3, ns, ck, 128), bf16), pltpu.VMEM((3, ns, ck, 128), bf16),
            pltpu.VMEM((3, ck, 128), bf16), pltpu.VMEM((3, nz, ck, 128), bf16),
            pltpu.VMEM((3, ns, ck, 128), bf16),
            dma((5, rows)), dma((5, rows)), dma((5, 2)), dma((5, 2)),
            dma((3, ns)), dma((3, ns)), dma((3, nz)), dma((3, nz)), dma((3, ns)), dma((3, ns)),
        ],
        compiler_params=pltpu.CompilerParams(
            collective_id=0, has_side_effects=True, vmem_limit_bytes=60 * 1024 * 1024),
    )(g, x, c, wt, wc)
    return (jnp.transpose(ig, (1, 0, 2))[None], jnp.transpose(cg, (0, 2, 1, 3)), weight_grad * scale)


def solution(mesh):
    placed = (
        P("tm", None, "space", None),
        P(None, "tm", "space", None),
        P("tm", None, "space", None),
        P(),
    )
    return jax.shard_map(
        functools.partial(per_device, mesh.shape["tm"], mesh.shape["space"]),
        mesh=mesh,
        in_specs=placed,
        out_specs=(P("tm", None, "space", None), P(None, "tm", "space", None), P()),
        check_vma=False,
    )
```

profile of v0, /device:TPU:0, one launch (start us, length us, event | category | flops | bytes accessed | tf_op | source)
XLA Modules:
  0.0 98.8 jit_solution(16636803604905877843)
XLA Ops:
  0.6 0.0 copy-start
  0.6 1.9 %copy.25 = bf16[2,24,4,1280]{3,1,2,0:T(8,128)(2,1)} copy(bf16[2,24,4,1280]{3,2,1,0:T(4,128)(2,1)} %param.5) | data formatting | bytes 983040 | tf_op args[1]
  2.6 0.0 copy-done
  2.7 0.2 constant_dynamic-slice_fusion
  2.9 0.8 copy.21.wc_ref
  3.7 0.0 copy-start.2
  3.7 0.0 copy-start.3
  3.7 1.1 %copy.18.wt_ref = bf16[3,96,864]{2,1,0:T(8,128)(2,1)} copy(bf16[3,96,864]{1,2,0:T(8,128)(2,1)S(1)} %bitcast.20) | data formatting | bytes 995328 | tf_op jit(solution)/shard_map/reshape | solution.py:436
  4.8 0.1 copy-done.2
  4.9 0.5 copy-done.3
  5.4 1.5 %copy_bitcast_fusion = (bf16[4,96,1280]{2,1,0:T(8,128)(2,1)}, bf16[4,96,1280]{2,1,0:T(8,128)(2,1)}) fusion(bf16[1,96,4,1280]{3,2,1,0:T(4,128)(2,1)S(1)} %copy-done.2, bf16[1,96,4,1280]{3,2,1,0:T(4,128)(2,1)S(1)} %copy-done.3), kind=kLoop, calls=%fused_computation | loop fusion | bytes 3932160 | tf_op jit(solution)/shard_map/transpose | solution.py:434
  6.8 86.7 %shard_map.67 = (bf16[4,96,1280]{2,1,0:T(8,128)(2,1)}, bf16[2,4,24,1280]{3,2,1,0:T(8,128)(2,1)}, f32[3,3,3,96,96]{4,3,2,1,0:T(8,128)}) custom-call(bf16[4,96,1280]{2,1,0:T(8,128)(2,1)} %get-tuple-element.16.g_ref, bf16[4,96,1280]{2,1,0:T(8,128)(2,1)} %get-tuple-element.15.x_ref, bf16[2,4,24,1280]{3,2,1,0:T(8,128)(2,1)} %bitcast.21, ...), custom_call_target="tpu_custom_call" | custom-call | tf_op jit(solution)/shard_map/pallas_call | solution.py:442
  93.6 0.0 copy-start.4
  93.6 0.0 copy-start.1
  93.6 3.0 %copy.19 = bf16[1,96,4,1280]{3,2,1,0:T(4,128)(2,1)} copy(bf16[1,96,4,1280]{3,1,2,0:T(8,128)(2,1)} %bitcast.23) | data formatting | bytes 1966080
  96.6 0.0 copy-done.4
  96.6 1.0 copy.20
  97.6 0.0 copy-done.1
  97.6 1.2 %broadcast_multiply_fusion = f32[3,3,3,96,96]{4,3,2,1,0:T(8,128)} fusion(f32[3,3,3,96,96]{4,3,2,1,0:T(8,128)S(1)} %copy-done.1), kind=kLoop, calls=%fused_computation.2 | loop fusion | flops 248832 | bytes 1990656 | tf_op jit(solution)/shard_map/mul | solution.py:468
  (3 shorter events, 0.1 us)
Async XLA Ops:
  0.6 1.9 %copy-start = (bf16[3,3,3,96,96]{4,3,2,1,0:T(8,128)(2,1)S(1)}, bf16[3,3,3,96,96]{4,3,2,1,0:T(8,128)(2,1)}, u32[]{:S(2)}) copy-start(bf16[3,3,3,96,96]{4,3,2,1,0:T(8,128)(2,1)} %param.7) | copy-start | bytes 1492996
  3.7 1.2 %copy-start.2 = (bf16[1,96,4,1280]{3,2,1,0:T(4,128)(2,1)S(1)}, bf16[1,96,4,1280]{3,2,1,0:T(4,128)(2,1)}, u32[]{:S(2)}) copy-start(bf16[1,96,4,1280]{3,2,1,0:T(4,128)(2,1)} %param.4) | copy-start | bytes 2949124
  3.7 1.7 %copy-start.3 = (bf16[1,96,4,1280]{3,2,1,0:T(4,128)(2,1)S(1)}, bf16[1,96,4,1280]{3,2,1,0:T(4,128)(2,1)}, u32[]{:S(2)}) copy-start(bf16[1,96,4,1280]{3,2,1,0:T(4,128)(2,1)} %param.6) | copy-start | bytes 2949124
  93.6 3.1 %copy-start.4 = (bf16[2,4,24,1280]{3,2,1,0:T(8,128)(2,1)S(1)}, bf16[2,4,24,1280]{3,2,1,0:T(8,128)(2,1)}, u32[]{:S(2)}) copy-start(bf16[2,4,24,1280]{3,2,1,0:T(8,128)(2,1)} %get-tuple-element.7) | copy-start | bytes 1474564
  93.6 4.0 %copy-start.1 = (f32[3,3,3,96,96]{4,3,2,1,0:T(8,128)S(1)}, f32[3,3,3,96,96]{4,3,2,1,0:T(8,128)}, u32[]{:S(2)}) copy-start(f32[3,3,3,96,96]{4,3,2,1,0:T(8,128)} %get-tuple-element.8) | copy-start | bytes 2985988
where the time goes:
time: 99 us; the launch traced here: 98.8 us
  Pallas kernels  86.7 us (88%)
  local copies, waits for them, and re-layouts  10.2 us (10%)
  other arithmetic  1.18 us (1%)
    pallas_call x1, Pallas kernels, per_device(): pl.pallas_call(functools.partial(kernel, nz, ns, ck, channels, share), ou...  86.7 us
    unnamed x14, local copies, waits for them, and re-layouts  7.34 us

commit v1 on v0

--- a/solution.py
+++ b/solution.py
@@ -14,17 +14,18 @@
 
 
 def kernel(
-    nz, ns, ck, channels, share,
-    g_ref, x_ref, c_ref, wt_ref, wc_ref, ig_ref, cg_ref, wg_ref,
+    nz, ns, ck, channels, share, scale,
+    g_hbm, x_hbm, c_hbm, w_hbm, ig_ref, cg_ref, wg_ref,
+    g_ref, x_ref, c_ref, w_ref, wf,
     gp, sc, dacc, wtmp, acc, xs_ref, wl_ref,
     sb, rb, zs, zb, gb,
-    z_send, z_recv, h_send, h_recv,
+    loads, z_send, z_recv, h_send, h_recv,
     rs_send, rs_recv, zz_send, zz_recv, ag_send, ag_recv,
 ):
     assert nz == 4
     j = lax.axis_index("tm")
     s = lax.axis_index("space")
-    rows, _, cols = g_ref.shape
+    _, rows, cols = g_ref.shape
     k_row = 3 * channels
     taps = 3 * k_row
     last = nz - 1
@@ -32,15 +33,32 @@
     high = 128
     late = jnp.where(j < last - 1, N2, C1)
 
+    fetch = [
+        pltpu.make_async_copy(src, dst, loads.at[n])
+        for n, (src, dst) in enumerate(((g_hbm, g_ref), (w_hbm, w_ref), (x_hbm, x_ref), (c_hbm, c_ref)))]
+    for copy in fetch:
+        copy.start()
+
     barrier = pltpu.get_barrier_semaphore()
     for k in range(1, ns):
         pl.semaphore_signal(barrier, inc=1, device_id={"space": lax.rem(s + k, ns)}, device_id_type=MESH)
     for k in range(1, nz):
         pl.semaphore_signal(barrier, inc=1, device_id={"tm": lax.rem(j + k, nz)}, device_id_type=MESH)
+    slab = 16
+
+    def turned(ref, at):
+        return jnp.transpose(ref[pl.ds(pl.multiple_of(at, slab), slab)], (1, 0, 2))
+
+    def turn_g(i, carry):
+        gp[OWN, 1:rows + 1, pl.ds(pl.multiple_of(i * slab, slab), slab), :] = turned(g_ref, i * slab)
+        return carry
+
+    fetch[0].wait()
+    lax.fori_loop(0, channels // slab, turn_g, 0)
     pl.semaphore_wait(barrier, ns - 1 + nz - 1)
 
     def row_copy(stream, slot_from, slot_to, r, target):
-        src = g_ref.at[r] if slot_from == OWN else gp.at[slot_from, r + 1]
+        src = gp.at[slot_from, r + 1]
         return pltpu.make_async_remote_copy(
             src_ref=src, dst_ref=gp.at[slot_to, r + 1],
             send_sem=z_send.at[stream, r], recv_sem=z_recv.at[slot_to, r],
@@ -73,14 +91,14 @@
     pl.when(j == 1)(lambda: own_c1(order[0]).start())
 
     def halo_up(slot):
-        src = g_ref.at[0] if slot is OWN else gp.at[slot, 1]
+        src = gp.at[slot, 1]
         return pltpu.make_async_remote_copy(
             src_ref=src, dst_ref=gp.at[slot, rows + 1],
             send_sem=h_send.at[slot, 0], recv_sem=h_recv.at[slot, 0],
             device_id={"space": lax.rem(s + ns - 1, ns)}, device_id_type=MESH)
 
     def halo_down(slot):
-        src = g_ref.at[rows - 1] if slot is OWN else gp.at[slot, rows]
+        src = gp.at[slot, rows]
         return pltpu.make_async_remote_copy(
             src_ref=src, dst_ref=gp.at[slot, 0],
             send_sem=h_send.at[slot, 1], recv_sem=h_recv.at[slot, 1],
@@ -116,28 +134,41 @@
         for slot in range(5):
             gp[slot, rows + 1] = jnp.zeros(gp.shape[2:], gp.dtype)
 
-    for r in range(rows):
-        gp[OWN, r + 1] = g_ref[r]
     wtmp[...] = jnp.zeros_like(wtmp)
     acc[...] = jnp.zeros_like(acc)
     stack = xs_ref.shape[1]
     xs_ref[:, channels:, :] = jnp.zeros((rows, stack - channels, cols), xs_ref.dtype)
     wl_ref[:, channels:, :] = jnp.zeros((5, stack - channels, taps), wl_ref.dtype)
-    for h in range(rows):
-        xs_ref[h, :channels, :] = x_ref[h]
-        xs_ref[h, channels:channels + share, :] = c_ref[0, h]
-        xs_ref[h, high:high + share, :] = c_ref[1, h]
+    fetch[1].wait()
     for slot, tap in ((OWN, 2), (N1, 1), (N2, 0)):
-        wl_ref[slot, :channels, :] = wt_ref[tap]
+        flipped = jnp.concatenate(
+            [w_ref[tap, (2 - b) * k_row:(3 - b) * k_row, :].astype(jnp.float32) for b in range(3)], axis=0)
+        across_taps = flipped.T
+        if tap < 2:
+            wf[tap] = across_taps
+        wl_ref[slot, :channels, :] = across_taps.astype(jnp.bfloat16)
+
+    def share_of(tap):
+        return wf[tap, pl.ds(pl.multiple_of(j * share, 8), share), :].astype(jnp.bfloat16)
+
+    def turn_x(i, carry):
+        xs_ref[:, pl.ds(pl.multiple_of(i * slab, slab), slab), :] = turned(x_ref, i * slab)
+        return carry
+
+    fetch[2].wait()
+    lax.fori_loop(0, channels // slab, turn_x, 0)
+    fetch[3].wait()
+    xs_ref[:, channels:channels + share, :] = jnp.transpose(c_ref[0], (1, 0, 2))
+    xs_ref[:, high:high + share, :] = jnp.transpose(c_ref[1], (1, 0, 2))
     for slot in (C1, C0):
         wl_ref[slot, :channels, :] = jnp.zeros((channels, taps), wl_ref.dtype)
 
     def weights_g0(slot):
-        wl_ref[slot, channels:channels + share, :] = wc_ref[0]
-        wl_ref[slot, high:high + share, :] = wc_ref[1]
+        wl_ref[slot, channels:channels + share, :] = share_of(0)
+        wl_ref[slot, high:high + share, :] = share_of(1)
 
     def weights_g1(slot):
-        wl_ref[slot, high:high + share, :] = wc_ref[0]
+        wl_ref[slot, high:high + share, :] = share_of(0)
 
     @pl.when(j == 0)
     def _():
@@ -276,7 +307,7 @@
             for b in range(3):
                 for d in range(3):
                     at = (b * 3 + d) * channels
-                    wg_ref[index, 2 - b, d] = acc[index, at:at + channels, :channels]
+                    wg_ref[index, 2 - b, d] = acc[index, at:at + channels, :channels] * scale
             for k in range(1, ns):
                 rs_copy(k).wait_send()
                 ag_copy(k).wait_send()
@@ -383,10 +414,15 @@
     steps[0][scatter]()
     steps[2][gather]()
     steps[1][gather]()
-    for h in range(rows):
-        ig_ref[h] = dacc[h, :channels, :].astype(jnp.bfloat16)
-        cg_ref[0, h] = dacc[h, channels:channels + share, :].astype(jnp.bfloat16)
-        cg_ref[1, h] = dacc[h, high:high + share, :].astype(jnp.bfloat16)
+
+    def turn_out(i, carry):
+        at = pl.ds(pl.multiple_of(i * slab, slab), slab)
+        ig_ref[at] = jnp.transpose(dacc[:, at, :].astype(jnp.bfloat16), (1, 0, 2))
+        return carry
+
+    lax.fori_loop(0, channels // slab, turn_out, 0)
+    cg_ref[0] = jnp.transpose(dacc[:, channels:channels + share, :].astype(jnp.bfloat16), (1, 0, 2))
+    cg_ref[1] = jnp.transpose(dacc[:, high:high + share, :].astype(jnp.bfloat16), (1, 0, 2))
     steps[0][across]()
     steps[2][finish]()
     steps[1][finish]()
@@ -424,31 +460,31 @@
 
 
 def per_device(nz, ns, frames, cache, grad_out, weight):
-    j = lax.axis_index("tm")
     _, channels, rows, cols = frames.shape
     share = cache.shape[1]
     taps = 9 * channels
     stack = 128 + up_to(share, 32)
     ck = up_to(-(-taps // ns), 16)
-    g = jnp.transpose(grad_out[0], (1, 0, 2))
-    x = jnp.transpose(frames[0], (1, 0, 2))
-    c = jnp.transpose(cache, (0, 2, 1, 3))
-    wt = jnp.transpose(weight[:, ::-1], (0, 4, 1, 2, 3)).reshape(3, channels, taps)
-    wc = lax.dynamic_slice_in_dim(wt[:2], j * share, share, axis=1)
     scale = 1.0 / math.sqrt(nz * ns * rows * cols)
     f32, bf16 = jnp.float32, jnp.bfloat16
     vmem = pl.BlockSpec(memory_space=pltpu.VMEM)
+    hbm = pl.BlockSpec(memory_space=pl.ANY)
     dma = pltpu.SemaphoreType.DMA
     ig, cg, weight_grad = pl.pallas_call(
-        functools.partial(kernel, nz, ns, ck, channels, share),
+        functools.partial(kernel, nz, ns, ck, channels, share, scale),
         out_shape=(
-            jax.ShapeDtypeStruct((rows, channels, cols), bf16),
-            jax.ShapeDtypeStruct((2, rows, share, cols), bf16),
+            jax.ShapeDtypeStruct(frames.shape[1:], bf16),
+            jax.ShapeDtypeStruct(cache.shape, bf16),
             jax.ShapeDtypeStruct(weight.shape, f32),
         ),
-        in_specs=[vmem] * 5,
+        in_specs=[hbm] * 4,
         out_specs=(vmem,) * 3,
         scratch_shapes=[
+            pltpu.VMEM(frames.shape[1:], bf16),
+            pltpu.VMEM(frames.shape[1:], bf16),
+            pltpu.VMEM(cache.shape, bf16),
+            pltpu.VMEM((3, taps, channels), bf16),
+            pltpu.VMEM((2, channels, taps), f32),
             pltpu.VMEM((5, rows + 2, channels, cols), bf16),
             pltpu.VMEM(((rows + 2) * 3 * channels, cols), bf16),
             pltpu.VMEM((rows, stack, cols), f32),
@@ -459,13 +495,14 @@
             pltpu.VMEM((3, ns, ck, 128), bf16), pltpu.VMEM((3, ns, ck, 128), bf16),
             pltpu.VMEM((3, ck, 128), bf16), pltpu.VMEM((3, nz, ck, 128), bf16),
             pltpu.VMEM((3, ns, ck, 128), bf16),
+            dma((4,)),
             dma((5, rows)), dma((5, rows)), dma((5, 2)), dma((5, 2)),
             dma((3, ns)), dma((3, ns)), dma((3, nz)), dma((3, nz)), dma((3, ns)), dma((3, ns)),
         ],
         compiler_params=pltpu.CompilerParams(
             collective_id=0, has_side_effects=True, vmem_limit_bytes=60 * 1024 * 1024),
-    )(g, x, c, wt, wc)
-    return (jnp.transpose(ig, (1, 0, 2))[None], jnp.transpose(cg, (0, 2, 1, 3)), weight_grad * scale)
+    )(grad_out[0], frames[0], cache, weight.reshape(3, taps, channels))
+    return ig[None], cg, weight_grad
 
 
 def solution(mesh):

time: 99 us -> 90.2 us (0.911)
  local copies, waits for them, and re-layouts: 10.2 us -> 4.46 us
  Pallas kernels: 86.7 us -> 84.9 us
  other arithmetic: 1.18 us -> 0 us
    unnamed x14 -> x7, local copies, waits for them, and re-layouts: 7.34 us -> 4.46 us
    pallas_call x1, Pallas kernels: 86.7 us -> 84.9 us  [per_device(): pl.pallas_call(functools.partial(kernel, nz, ns, ck, channels, share, sca...]
    transpose x2 -> x0, local copies, waits for them, and re-layouts: 1.51 us -> none  [the longest x1 1.46 us: per_device(): x = jnp.transpose(frames[0], (1, 0, 2))]
    mul x1 -> x0, other arithmetic: 1.18 us -> none  [per_device(): weight_grad * scale]
    reshape x1 -> x0, local copies, waits for them, and re-layouts: 1.07 us -> none  [per_device(): jnp.transpose(weight[:, ::-1], (0, 4, 1, 2, 3)).reshape(3, channels, taps)]
where the time goes in v1:
time: 90.2 us; the launch traced here: 90.1 us
  Pallas kernels  84.9 us (94%)
  local copies, waits for them, and re-layouts  4.46 us (5%)
    pallas_call x1, Pallas kernels, per_device(): pl.pallas_call(functools.partial(kernel, nz, ns, ck, channels, share, sca...  84.9 us
    unnamed x7, local copies, waits for them, and re-layouts  4.46 us

profile of v1, /device:TPU:0, one launch (start us, length us, event | category | flops | bytes accessed | tf_op | source)
XLA Modules:
  0.0 90.1 jit_solution(621425788017034879)
XLA Ops:
  0.6 84.9 %shard_map.67 = (bf16[96,4,1280]{2,1,0:T(4,128)(2,1)}, bf16[2,24,4,1280]{3,2,1,0:T(4,128)(2,1)}, f32[3,3,3,96,96]{4,3,2,1,0:T(8,128)}) custom-call(bf16[96,4,1280]{2,1,0:T(4,128)(2,1)} %bitcast.4, bf16[96,4,1280]{2,1,0:T(4,128)(2,1)} %bitcast.5, bf16[2,24,4,1280]{3,2,1,0:T(4,128)(2,1)} %c_hbm.1, bf16[3,864,96]{2,1,0:T(8,128)(2,1)} %bitcast.7), custom_call_target="tpu_custom_call" | custom-call | tf_op jit(solution)/shard_map/pallas_call | solution.py:473
  85.6 0.0 copy-start.1
  85.6 0.0 copy-start
  85.6 2.6 %copy.10 = bf16[1,96,4,1280]{3,2,1,0:T(4,128)(2,1)} copy(bf16[1,96,4,1280]{3,2,1,0:T(4,128)(2,1)} %bitcast.6) | data formatting | bytes 1966080
  88.2 0.0 copy-done.1
  88.2 0.8 copy.11
  89.0 0.0 copy-done
  89.0 1.1 %copy.12 = f32[3,3,3,96,96]{4,3,2,1,0:T(8,128)} copy(f32[3,3,3,96,96]{4,3,2,1,0:T(8,128)S(1)} %copy-done) | data formatting | bytes 1990656
Async XLA Ops:
  85.6 2.6 %copy-start.1 = (bf16[2,24,4,1280]{3,2,1,0:T(4,128)(2,1)S(1)}, bf16[2,24,4,1280]{3,2,1,0:T(4,128)(2,1)}, u32[]{:S(2)}) copy-start(bf16[2,24,4,1280]{3,2,1,0:T(4,128)(2,1)} %get-tuple-element.13) | copy-start | bytes 1474564
  85.6 3.4 %copy-start = (f32[3,3,3,96,96]{4,3,2,1,0:T(8,128)S(1)}, f32[3,3,3,96,96]{4,3,2,1,0:T(8,128)}, u32[]{:S(2)}) copy-start(f32[3,3,3,96,96]{4,3,2,1,0:T(8,128)} %get-tuple-element.14) | copy-start | bytes 2985988

commit v2 on v1

v2 whole, which is shorter than its diff:
```python
import functools
import math

import jax
import jax.numpy as jnp
from jax import lax
from jax.experimental import pallas as pl
from jax.experimental.pallas import tpu as pltpu
from jax.sharding import PartitionSpec as P

MESH = pl.DeviceIdType.MESH
OWN, N1, LATE, C0 = range(4)
TO_PREV, FWD_PREV, TO_NEXT, FWD_C0 = range(4)
NT = (((1,), (1,)), ((), ()))
LANES = 128
F32, BF16 = jnp.float32, jnp.bfloat16


def kernel(
    nz, ns, ck, scale,
    g_hbm, x_hbm, c_hbm, w_hbm, ig_ref, cg_ref, wg_ref,
    g_ref, x_ref, c_ref, w_ref,
    gp, sc, xpad, cpad, dx, dc, wlx, wlc, wtx, wtc, flat,
    sb, rb, zs, zb, gb, cb, res_out, res_in,
    loads, z_send, z_recv, h_send, h_recv,
    rs_send, rs_recv, zz_send, zz_recv, ag_send, ag_recv, c_sem, res_sem,
):
    assert nz == 4
    j = lax.axis_index("tm")
    s = lax.axis_index("space")
    channels, rows, cols = g_ref.shape
    share = c_ref.shape[1]
    half = 2 * share
    assert channels == 2 * half and rows >= 4
    width = 3 * channels
    full, rem = width // LANES, width % LANES
    groups = LANES // rem
    part = width // groups
    assert full == 2 and LANES % rem == 0 and part % 8 == 0
    last = nz - 1
    order = [0, rows - 1, *range(1, rows - 1)]
    slab = 16
    prev = lax.rem(j + nz - 1, nz)
    nxt = lax.rem(j + 1, nz)

    def both(*terms):
        return functools.reduce(jnp.logical_and, terms)

    def ordered(i):
        return jnp.where(i == 0, 0, jnp.where(i == 1, rows - 1, i - 1))

    fetch_g, fetch_c, fetch_x, fetch_w = [
        pltpu.make_async_copy(src, dst, loads.at[n])
        for n, (src, dst) in enumerate(((g_hbm, g_ref), (c_hbm, c_ref), (x_hbm, x_ref), (w_hbm, w_ref)))]
    for copy in (fetch_g, fetch_c, fetch_x, fetch_w):
        copy.start()
    barrier = pltpu.get_barrier_semaphore()
    for k in range(1, ns):
        pl.semaphore_signal(barrier, inc=1, device_id={"space": lax.rem(s + k, ns)}, device_id_type=MESH)
    for k in range(1, nz):
        pl.semaphore_signal(barrier, inc=1, device_id={"tm": lax.rem(j + k, nz)}, device_id_type=MESH)

    def turned(ref, at):
        return jnp.transpose(ref[pl.ds(pl.multiple_of(at, slab), slab)], (1, 0, 2))

    def turn_g(i, carry):
        gp[OWN, 1:rows + 1, pl.ds(pl.multiple_of(i * slab, slab), slab), :] = turned(g_ref, i * slab)
        return carry

    fetch_g.wait()
    lax.fori_loop(0, channels // slab, turn_g, 0)
    fetch_c.wait()
    pl.semaphore_wait(barrier, ns - 1 + nz - 1)

    def row_copy(stream, slot_from, slot_to, r, target):
        return pltpu.make_async_remote_copy(
            src_ref=gp.at[slot_from, r + 1], dst_ref=gp.at[slot_to, r + 1],
            send_sem=z_send.at[stream, r], recv_sem=z_recv.at[slot_to, r],
            device_id={"tm": target}, device_id_type=MESH)

    def to_prev(r):
        return row_copy(TO_PREV, OWN, N1, r, prev)

    def fwd_prev(r):
        return row_copy(FWD_PREV, N1, LATE, r, prev)

    def own_c0(r):
        return row_copy(TO_NEXT, OWN, C0, r, nxt)

    def own_c1(r):
        return row_copy(TO_NEXT, OWN, LATE, r, nxt)

    def fwd_c0(r):
        return row_copy(FWD_C0, C0, C0, r, nxt)

    def cache_copy():
        return pltpu.make_async_remote_copy(
            src_ref=c_ref, dst_ref=cb, send_sem=c_sem.at[0], recv_sem=c_sem.at[1],
            device_id={"tm": prev}, device_id_type=MESH)

    def result_copy(f):
        return pltpu.make_async_remote_copy(
            src_ref=res_out.at[f], dst_ref=res_in.at[f], send_sem=res_sem.at[0, f], recv_sem=res_sem.at[1, f],
            device_id={"tm": nxt}, device_id_type=MESH)

    pl.when(j == last)(lambda: cache_copy().start())
    for i, r in enumerate(order):
        pl.when(j >= 1)(lambda: to_prev(r).start())
        pl.when(j == 0)(lambda: own_c0(r).start())
        if i < 2:
            pl.when(j == 1)(lambda: own_c1(r).start())

    def halo_up(slot):
        return pltpu.make_async_remote_copy(
            src_ref=gp.at[slot, 1], dst_ref=gp.at[slot, rows + 1],
            send_sem=h_send.at[slot, 0], recv_sem=h_recv.at[slot, 0],
            device_id={"space": lax.rem(s + ns - 1, ns)}, device_id_type=MESH)

    def halo_down(slot):
        return pltpu.make_async_remote_copy(
            src_ref=gp.at[slot, rows], dst_ref=gp.at[slot, 0],
            send_sem=h_send.at[slot, 1], recv_sem=h_recv.at[slot, 1],
            device_id={"space": lax.rem(s + 1, ns)}, device_id_type=MESH)

    def halo_start(slot, i):
        pl.when(both(i == 0, s >= 1))(lambda: halo_up(slot).start())
        pl.when(both(i == 1, s < ns - 1))(lambda: halo_down(slot).start())

    for i in range(2):
        halo_start(OWN, jnp.int32(i))

    edge = 2 * channels
    for ref in (xpad, cpad):
        ref[:edge, :] = jnp.zeros((edge, cols), BF16)
        ref[edge + rows * channels:, :] = jnp.zeros((edge, cols), BF16)
    dx[...] = jnp.zeros_like(dx)
    dc[...] = jnp.zeros_like(dc)
    wtx[...] = jnp.zeros_like(wtx)
    wtc[...] = jnp.zeros_like(wtc)
    used = full * width + part
    for tap in range(3):
        flat[tap, used:, :] = jnp.zeros((ns * ck - used, LANES), F32)

    def turn_x(i, carry):
        block = turned(x_ref, i * slab)
        for h in range(rows):
            xpad[pl.ds(pl.multiple_of((h + 2) * channels + i * slab, slab), slab), :] = block[h]
        return carry

    fetch_x.wait()
    lax.fori_loop(0, channels // slab, turn_x, 0)

    def turn_w(i, carry):
        at = pl.multiple_of(lax.rem(i, 3) * channels, slab)
        wlx[lax.div(i, 3), pl.ds(at, channels), :] = w_ref[i].astype(F32).T.astype(BF16)
        return carry

    fetch_w.wait()
    lax.fori_loop(0, 9, turn_w, 0)
    base = jnp.where(j < 2, 0, half)
    for b in range(3):
        at = b * channels
        near = pl.ds(pl.multiple_of(at + base, slab), half)
        wlc[0, at:at + half, :] = wlx[0, near, :]
        wlc[0, at + half:at + channels, :] = wlx[1, near, :]
        wlc[1, at:at + half, :] = jnp.zeros((half, width), BF16)
        wlc[1, at + half:at + channels, :] = wlx[0, near, :]

    def place_cache(lower, upper):
        nothing = jnp.zeros((rows, share, cols), F32)
        for f in range(2):
            low, high = [
                nothing if ref is None else jnp.transpose(ref[f].astype(F32), (1, 0, 2)) for ref in (lower, upper)]
            for h in range(rows):
                at = (h + 2) * channels + f * half
                cpad[at:at + half, :] = jnp.concatenate([low[h], high[h]], axis=0).astype(BF16)

    pl.when(j == 0)(lambda: place_cache(c_ref, None))
    pl.when(j == 1)(lambda: place_cache(None, c_ref))

    lane = lax.broadcasted_iota(jnp.int32, (channels, cols), 1)

    def shift(slot, p, to):
        value = gp[slot, p]
        wide = value.astype(F32)
        sc[to, :channels, :] = jnp.where(lane == cols - 1, 0.0, pltpu.roll(wide, cols - 1, 1)).astype(BF16)
        sc[to, channels:2 * channels, :] = value
        sc[to, 2 * channels:, :] = jnp.where(lane == 0, 0.0, pltpu.roll(wide, 1, 1)).astype(BF16)

    def kernel_sum(wt, pad, index, at, p):
        span = pl.ds(pl.multiple_of(p * channels, slab), width)
        wt[index, :, :width] += lax.dot_general(sc[at], pad[span, :], NT, preferred_element_type=F32)

    def data_sum(wl, out, index, at, p):
        span = pl.ds(pl.multiple_of(p * channels, slab), width)
        out[span, :] += jnp.dot(wl[index], sc[at], preferred_element_type=F32)

    def halo_sums(wt, pad, wl, out, index, at, side):
        h, b = (0, 2) if side == 0 else (rows - 1, 0)
        span = slice((h + 2) * channels, (h + 3) * channels)
        tap = slice(b * channels, (b + 1) * channels)
        wt[index, :, tap] += lax.dot_general(sc[at], pad[span, :], NT, preferred_element_type=F32)
        out[span, :] += jnp.dot(wl[index, tap, :], sc[at], preferred_element_type=F32)

    wide_lane = lax.broadcasted_iota(jnp.int32, (width, wtx.shape[2]), 1)
    in_lower = both(lax.rem(wide_lane, channels) < half, wide_lane < width)
    in_upper = both(lax.rem(wide_lane, channels) >= half, wide_lane < width)
    back = wtx.shape[2] - half

    def pack(tap):
        def put(total):
            for q in range(full):
                flat[tap, q * width:(q + 1) * width, :] = total[:, q * LANES:(q + 1) * LANES]
            tail = total[:, full * LANES:]
            packed = tail[:part]
            for k in range(1, groups):
                packed = packed + pltpu.roll(tail[k * part:(k + 1) * part], k * rem, 1)
            flat[tap, full * width:used, :] = packed

        own = wtx[tap]
        if tap == 2:
            put(own)
            return

        @pl.when(j < 2)
        def _():
            turned_c0 = pltpu.roll(wtc[0], back, 1)
            put(own + jnp.where(
                in_lower, turned_c0 if tap == 1 else wtc[0] + pltpu.roll(wtc[1], back, 1), 0.0))

        @pl.when(j >= 2)
        def _():
            put(own + jnp.where(in_upper, wtc[0] if tap == 1 else pltpu.roll(wtc[0], half, 1) + wtc[1], 0.0))

    def reduction(index):
        def rs_copy(k):
            to = lax.rem(s + k, ns)
            return pltpu.make_async_remote_copy(
                src_ref=sb.at[index, to], dst_ref=rb.at[index, s],
                send_sem=rs_send.at[index, k], recv_sem=rs_recv.at[index, s],
                device_id={"space": to}, device_id_type=MESH)

        def rs_landed(k):
            source = lax.rem(s + ns - k, ns)
            return pltpu.make_async_remote_copy(
                src_ref=sb.at[index, source], dst_ref=rb.at[index, source],
                send_sem=rs_send.at[index, k], recv_sem=rs_recv.at[index, source],
                device_id={"space": source}, device_id_type=MESH)

        def z_copy(k):
            return pltpu.make_async_remote_copy(
                src_ref=zs.at[index], dst_ref=zb.at[index, j],
                send_sem=zz_send.at[index, k], recv_sem=zz_recv.at[index, j],
                device_id={"tm": lax.rem(j + k, nz)}, device_id_type=MESH)

        def z_landed(k):
            source = lax.rem(j + nz - k, nz)
            return pltpu.make_async_remote_copy(
                src_ref=zs.at[index], dst_ref=zb.at[index, source],
                send_sem=zz_send.at[index, k], recv_sem=zz_recv.at[index, source],
                device_id={"tm": source}, device_id_type=MESH)

        def ag_copy(k):
            return pltpu.make_async_remote_copy(
                src_ref=gb.at[index, s], dst_ref=gb.at[index, s],
                send_sem=ag_send.at[index, k], recv_sem=ag_recv.at[index, s],
                device_id={"space": lax.rem(s + k, ns)}, device_id_type=MESH)

        def ag_landed(k):
            source = lax.rem(s + ns - k, ns)
            return pltpu.make_async_remote_copy(
                src_ref=gb.at[index, source], dst_ref=gb.at[index, source],
                send_sem=ag_send.at[index, k], recv_sem=ag_recv.at[index, source],
                device_id={"space": source}, device_id_type=MESH)

        def scatter():
            pack(index)
            for q in range(ns):
                sb[index, q] = flat[index, q * ck:(q + 1) * ck, :].astype(BF16)
            for k in range(1, ns):
                rs_copy(k).start()

        def across():
            total = flat[index, pl.ds(pl.multiple_of(s * ck, slab), ck), :]
            for k in range(1, ns):
                rs_landed(k).wait_recv()
                total = total + rb[index, lax.rem(s + ns - k, ns)].astype(F32)
            zs[index] = total.astype(BF16)

        def exchange():
            for k in range(1, nz):
                z_copy(k).start()

        def gather():
            zb[index, j] = zs[index]
            for k in range(1, nz):
                z_landed(k).wait_recv()
            total = zb[index, 0].astype(F32)
            for q in range(1, nz):
                total = total + zb[index, q].astype(F32)
            gb[index, s] = total.astype(BF16)
            for k in range(1, ns):
                ag_copy(k).start()

        def finish():
            for k in range(1, ns):
                ag_landed(k).wait_recv()
            for q in range(ns):
                flat[index, q * ck:(q + 1) * ck, :] = gb[index, q].astype(F32) * scale
            first = flat[index, :width, :]
            second = flat[index, width:2 * width, :]
            packed = flat[index, 2 * width:used, :]
            at = lax.broadcasted_iota(jnp.int32, (width, LANES), 1)
            step = LANES - channels
            middle = jnp.where(at < step, pltpu.roll(first, step, 1), pltpu.roll(second, step, 1))
            third = jnp.concatenate(
                [pltpu.roll(packed, (2 * step - k * rem) % LANES, 1) if (2 * step - k * rem) % LANES else packed
                 for k in range(groups)], axis=0)
            final = jnp.where(at < 2 * step, pltpu.roll(second, 2 * step, 1), third)
            for b, value in enumerate((first, middle, final)):
                wg_ref[index, b] = value[:, :channels]

        def sent():
            for k in range(1, ns):
                rs_copy(k).wait_send()
                ag_copy(k).wait_send()
            for k in range(1, nz):
                z_copy(k).wait_send()

        return scatter, across, exchange, gather, finish, sent

    steps = [reduction(tap) for tap in range(3)]
    scatter, across, exchange, gather, finish, sent = range(6)

    def middle_row(e):
        r = ordered(e)

        @pl.when(j < last)
        def _():
            row_copy(TO_PREV, OWN, N1, r, prev).wait_recv()
            pl.when(j >= 1)(lambda: fwd_prev(r).start())
            halo_start(N1, e)

        @pl.when(both(j >= 1, j < last))
        def _():
            row_copy(TO_NEXT, OWN, C0, r, nxt).wait_recv()
            pl.when(j == 1)(lambda: fwd_c0(r).start())
            halo_start(C0, e)

        @pl.when(both(j == 1, e == rows - 1))
        def _():
            for q in order[2:]:
                own_c1(q).start()

    def late_row(e):
        @pl.when(j < last)
        def _():
            row_copy(FWD_PREV, N1, LATE, ordered(e), prev).wait_recv()
            halo_start(LATE, e)

    def halo_wait(slot, side):
        if side == 0:
            halo_up(slot).wait_send()
            halo_down(slot).wait_recv()
        else:
            halo_down(slot).wait_send()
            halo_up(slot).wait_recv()

    ahead = jnp.where(j < 2, 1, 0)

    def results(f, offset):
        rows_of = [
            dc[pl.ds(pl.multiple_of((h + 2) * channels + f * half + offset, 8), share), :] for h in range(rows)]
        return jnp.transpose(jnp.stack(rows_of, axis=0).astype(BF16), (1, 0, 2))

    def step(n, carry):
        phase = lax.div(n, rows)
        i = lax.rem(n, rows)
        r = ordered(i)

        @pl.when(both(n >= rows, n + ahead < 2 * rows))
        def _():
            middle_row(n + ahead - rows)

        pl.when(phase == 2)(lambda: late_row(i))

        @pl.when(both(n == rows, j == 2))
        def _():
            cache_copy().wait_recv()
            place_cache(c_ref, cb)

        with_x = jnp.logical_or(phase == 0, jnp.logical_or(both(phase == 1, j < last), j < 2))
        x_slot = phase
        tap = 2 - phase
        with_c = jnp.logical_or(
            both(phase == 0, j < 2), jnp.logical_or(both(phase == 1, j < last), both(phase == 2, j == 2)))
        apart = both(phase >= 1, j >= 1)
        c_slot = jnp.where(apart, jnp.where(phase == 1, C0, LATE), phase)
        c_kind = jnp.where(phase == 0, j, jnp.where(both(phase == 1, j >= 1), 0, 1))
        c_at = jnp.where(apart, 1, 0)

        @pl.when(with_x)
        def _():
            shift(x_slot, r + 1, 0)
            kernel_sum(wtx, xpad, tap, 0, r + 1)
            data_sum(wlx, dx, tap, 0, r + 1)

        @pl.when(with_c)
        def _():
            pl.when(apart)(lambda: shift(c_slot, r + 1, 1))
            kernel_sum(wtc, cpad, c_kind, c_at, r + 1)
            data_sum(wlc, dc, c_kind, c_at, r + 1)

        pl.when(both(n == 2, j < 2))(lambda: middle_row(jnp.int32(0)))

        @pl.when(i == 2)
        def _():
            for side in range(2):
                p = 0 if side == 0 else rows + 1

                @pl.when(s >= 1 if side == 0 else s < ns - 1)
                def _():
                    @pl.when(with_x)
                    def _():
                        halo_wait(x_slot, side)
                        shift(x_slot, p, 0)
                        halo_sums(wtx, xpad, wlx, dx, tap, 0, side)

                    @pl.when(with_c)
                    def _():
                        @pl.when(apart)
                        def _():
                            halo_wait(c_slot, side)
                            shift(c_slot, p, 1)

                        halo_sums(wtc, cpad, wlc, dc, c_kind, c_at, side)

        pl.when(n == rows - 1)(steps[2][scatter])

        @pl.when(n == 2 * rows - 1)
        def _():
            steps[1][scatter]()

            @pl.when(j == 2)
            def _():
                res_out[0] = results(0, share)
                result_copy(0).start()

        return carry

    lax.fori_loop(0, 3 * rows - 1, step, 0)
    steps[2][across]()
    steps[1][across]()

    final = jnp.int32(rows - 1)
    p = order[-1] + 1
    late_row(final)

    @pl.when(j < 2)
    def _():
        shift(LATE, p, 0)
        kernel_sum(wtx, xpad, 0, 0, p)

    @pl.when(j == 2)
    def _():
        shift(LATE, p, 1)
        kernel_sum(wtc, cpad, 1, 1, p)

    steps[0][scatter]()
    steps[2][exchange]()
    steps[1][exchange]()

    @pl.when(j == 2)
    def _():
        data_sum(wlc, dc, 1, 1, p)
        res_out[1] = results(1, share)
        result_copy(1).start()

    pl.when(j < 2)(lambda: data_sum(wlx, dx, 0, 0, p))

    def turn_out(i, carry):
        block = [
            dx[pl.ds(pl.multiple_of((h + 2) * channels + i * slab, slab), slab), :] for h in range(rows)]
        ig_ref[pl.ds(pl.multiple_of(i * slab, slab), slab)] = jnp.transpose(
            jnp.stack(block, axis=0).astype(BF16), (1, 0, 2))
        return carry

    lax.fori_loop(0, channels // slab, turn_out, 0)

    @pl.when(j < last)
    def _():
        offset = jnp.where(j == 1, share, 0)
        for f in range(2):
            cg_ref[f] = results(f, offset)

    steps[0][across]()
    steps[0][exchange]()
    steps[2][gather]()
    steps[1][gather]()
    steps[0][gather]()
    steps[2][finish]()
    steps[1][finish]()

    @pl.when(j == last)
    def _():
        for f in range(2):
            result_copy(f).wait_recv()
            cg_ref[f] = res_in[f]
        cache_copy().wait_send()

    @pl.when(j == 2)
    def _():
        for f in range(2):
            result_copy(f).wait_send()

    for r in range(rows):
        pl.when(j >= 1)(lambda: to_prev(r).wait_send())
        pl.when(both(j >= 1, j < last))(lambda: fwd_prev(r).wait_send())
        pl.when(j == 0)(lambda: own_c0(r).wait_send())

        @pl.when(j == 1)
        def _():
            own_c1(r).wait_send()
            fwd_c0(r).wait_send()

    for tap in range(3):
        steps[tap][sent]()
    steps[0][finish]()


def up_to(value, step):
    return -(-value // step) * step


def per_device(nz, ns, frames, cache, grad_out, weight):
    _, channels, rows, cols = frames.shape
    width = 3 * channels
    wide = up_to(width, LANES)
    ck = up_to(-(-(width * channels * 3) // (ns * LANES)), 16)
    scale = 1.0 / math.sqrt(nz * ns * rows * cols)
    vmem = pl.BlockSpec(memory_space=pltpu.VMEM)
    hbm = pl.BlockSpec(memory_space=pl.ANY)
    dma = pltpu.SemaphoreType.DMA
    padded = (rows + 4) * channels
    ig, cg, weight_grad = pl.pallas_call(
        functools.partial(kernel, nz, ns, ck, scale),
        out_shape=(
            jax.ShapeDtypeStruct(frames.shape[1:], BF16),
            jax.ShapeDtypeStruct(cache.shape, BF16),
            jax.ShapeDtypeStruct((3, 3, width, channels), F32),
        ),
        in_specs=[hbm] * 4,
        out_specs=(vmem,) * 3,
        scratch_shapes=[
            pltpu.VMEM(frames.shape[1:], BF16),
            pltpu.VMEM(frames.shape[1:], BF16),
            pltpu.VMEM(cache.shape, BF16),
            pltpu.VMEM((9, width, channels), BF16),
            pltpu.VMEM((4, rows + 2, channels, cols), BF16),
            pltpu.VMEM((2, width, cols), BF16),
            pltpu.VMEM((padded, cols), BF16), pltpu.VMEM((padded, cols), BF16),
            pltpu.VMEM((padded, cols), F32), pltpu.VMEM((padded, cols), F32),
            pltpu.VMEM((3, width, width), BF16), pltpu.VMEM((2, width, width), BF16),
            pltpu.VMEM((3, width, wide), F32), pltpu.VMEM((2, width, wide), F32),
            pltpu.VMEM((3, ns * ck, LANES), F32),
            pltpu.VMEM((3, ns, ck, LANES), BF16), pltpu.VMEM((3, ns, ck, LANES), BF16),
            pltpu.VMEM((3, ck, LANES), BF16), pltpu.VMEM((3, nz, ck, LANES), BF16),
            pltpu.VMEM((3, ns, ck, LANES), BF16),
            pltpu.VMEM(cache.shape, BF16), pltpu.VMEM(cache.shape, BF16), pltpu.VMEM(cache.shape, BF16),
            dma((4,)),
            dma((4, rows)), dma((4, rows)), dma((4, 2)), dma((4, 2)),
            dma((3, ns)), dma((3, ns)), dma((3, nz)), dma((3, nz)), dma((3, ns)), dma((3, ns)),
            dma((2,)), dma((2, 2)),
        ],
        compiler_params=pltpu.CompilerParams(
            collective_id=0, has_side_effects=True, vmem_limit_bytes=60 * 1024 * 1024),
    )(grad_out[0], frames[0], cache, weight.reshape(9, width, channels))
    return ig[None], cg, weight_grad.reshape(weight.shape)


def solution(mesh):
    placed = (
        P("tm", None, "space", None),
        P(None, "tm", "space", None),
        P("tm", None, "space", None),
        P(),
    )
    return jax.shard_map(
        functools.partial(per_device, mesh.shape["tm"], mesh.shape["space"]),
        mesh=mesh,
        in_specs=placed,
        out_specs=(P("tm", None, "space", None), P(None, "tm", "space", None), P()),
        check_vma=False,
    )
```

time: 90.2 us -> 73.2 us (0.81)
  the two profiles are of different devices: /device:TPU:0 before, /device:TPU:25 now
where the time goes in v2:
time: 73.2 us; the launch traced here: 73 us
  Pallas kernels  67.9 us (93%)
  local copies, waits for them, and re-layouts  4.46 us (6%)
    pallas_call x1, Pallas kernels, per_device(): pl.pallas_call(functools.partial(kernel, nz, ns, ck, scale), out_shape=(j...  67.9 us
    unnamed x7, local copies, waits for them, and re-layouts  4.46 us

profile of v2, /device:TPU:25, one launch (start us, length us, event | category | flops | bytes accessed | tf_op | source)
XLA Modules:
  0.0 73.0 jit_solution(11058250189232191542)
XLA Ops:
  0.6 67.9 %shard_map.67 = (bf16[96,4,1280]{2,1,0:T(4,128)(2,1)}, bf16[2,24,4,1280]{3,2,1,0:T(4,128)(2,1)}, f32[3,3,288,96]{3,2,1,0:T(8,128)}) custom-call(bf16[96,4,1280]{2,1,0:T(4,128)(2,1)} %bitcast.6, bf16[96,4,1280]{2,1,0:T(4,128)(2,1)} %bitcast.7, bf16[2,24,4,1280]{3,2,1,0:T(4,128)(2,1)} %c_hbm.1, bf16[9,288,96]{2,1,0:T(8,128)(2,1)} %bitcast.9), custom_call_target="tpu_custom_call" | custom-call | tf_op jit(solution)/shard_map/pallas_call | solution.py:545
  68.5 0.0 copy-start.1
  68.6 0.0 copy-start
  68.6 2.6 %copy.10 = bf16[1,96,4,1280]{3,2,1,0:T(4,128)(2,1)} copy(bf16[1,96,4,1280]{3,2,1,0:T(4,128)(2,1)} %bitcast.8) | data formatting | bytes 1966080
  71.2 0.0 copy-done.1
  71.2 0.8 %copy.11 = bf16[2,24,4,1280]{3,2,1,0:T(4,128)(2,1)} copy(bf16[2,24,4,1280]{3,2,1,0:T(4,128)(2,1)S(1)} %copy-done.1) | data formatting | bytes 983040
  72.0 0.0 copy-done
  72.0 1.1 %copy.12 = f32[3,3,3,96,96]{4,3,2,1,0:T(8,128)} copy(f32[3,3,3,96,96]{4,3,2,1,0:T(8,128)S(1)} %bitcast.5) | data formatting | bytes 1990656
Async XLA Ops:
  68.5 2.6 %copy-start.1 = (bf16[2,24,4,1280]{3,2,1,0:T(4,128)(2,1)S(1)}, bf16[2,24,4,1280]{3,2,1,0:T(4,128)(2,1)}, u32[]{:S(2)}) copy-start(bf16[2,24,4,1280]{3,2,1,0:T(4,128)(2,1)} %get-tuple-element.13) | copy-start | bytes 1474564
  68.6 3.4 %copy-start = (f32[3,3,288,96]{3,2,1,0:T(8,128)S(1)}, f32[3,3,288,96]{3,2,1,0:T(8,128)}, u32[]{:S(2)}) copy-start(f32[3,3,288,96]{3,2,1,0:T(8,128)} %get-tuple-element.8) | copy-start | bytes 2985988

commit v3 on v2

--- a/solution.py
+++ b/solution.py
@@ -17,13 +17,13 @@
 
 
 def kernel(
-    nz, ns, ck, scale,
-    g_hbm, x_hbm, c_hbm, w_hbm, ig_ref, cg_ref, wg_ref,
-    g_ref, x_ref, c_ref, w_ref,
+    nz, ns, ck,
+    g_hbm, x_hbm, c_hbm, w_hbm, ig_hbm, cg_hbm, gb,
+    ig_ref, cg_ref, g_ref, x_ref, c_ref, w_ref,
     gp, sc, xpad, cpad, dx, dc, wlx, wlc, wtx, wtc, flat,
-    sb, rb, zs, zb, gb, cb, res_out, res_in,
+    sb, rb, zs, zb, mine, cb, res_out, res_in,
     loads, z_send, z_recv, h_send, h_recv,
-    rs_send, rs_recv, zz_send, zz_recv, ag_send, ag_recv, c_sem, res_sem,
+    rs_send, rs_recv, zz_send, zz_recv, ag_send, ag_recv, c_sem, res_sem, stores,
 ):
     assert nz == 4
     j = lax.axis_index("tm")
@@ -262,14 +262,14 @@
 
         def ag_copy(k):
             return pltpu.make_async_remote_copy(
-                src_ref=gb.at[index, s], dst_ref=gb.at[index, s],
+                src_ref=mine.at[index], dst_ref=gb.at[index, s],
                 send_sem=ag_send.at[index, k], recv_sem=ag_recv.at[index, s],
                 device_id={"space": lax.rem(s + k, ns)}, device_id_type=MESH)
 
         def ag_landed(k):
             source = lax.rem(s + ns - k, ns)
             return pltpu.make_async_remote_copy(
-                src_ref=gb.at[index, source], dst_ref=gb.at[index, source],
+                src_ref=mine.at[index], dst_ref=gb.at[index, source],
                 send_sem=ag_send.at[index, k], recv_sem=ag_recv.at[index, source],
                 device_id={"space": source}, device_id_type=MESH)
 
@@ -298,27 +298,18 @@
             total = zb[index, 0].astype(F32)
             for q in range(1, nz):
                 total = total + zb[index, q].astype(F32)
-            gb[index, s] = total.astype(BF16)
+            mine[index] = total.astype(BF16)
             for k in range(1, ns):
                 ag_copy(k).start()
+            keep().start()
+
+        def keep():
+            return pltpu.make_async_copy(mine.at[index], gb.at[index, s], stores.at[index])
 
         def finish():
             for k in range(1, ns):
                 ag_landed(k).wait_recv()
-            for q in range(ns):
-                flat[index, q * ck:(q + 1) * ck, :] = gb[index, q].astype(F32) * scale
-            first = flat[index, :width, :]
-            second = flat[index, width:2 * width, :]
-            packed = flat[index, 2 * width:used, :]
-            at = lax.broadcasted_iota(jnp.int32, (width, LANES), 1)
-            step = LANES - channels
-            middle = jnp.where(at < step, pltpu.roll(first, step, 1), pltpu.roll(second, step, 1))
-            third = jnp.concatenate(
-                [pltpu.roll(packed, (2 * step - k * rem) % LANES, 1) if (2 * step - k * rem) % LANES else packed
-                 for k in range(groups)], axis=0)
-            final = jnp.where(at < 2 * step, pltpu.roll(second, 2 * step, 1), third)
-            for b, value in enumerate((first, middle, final)):
-                wg_ref[index, b] = value[:, :channels]
+            keep().wait()
 
         def sent():
             for k in range(1, ns):
@@ -474,7 +465,6 @@
     def _():
         data_sum(wlc, dc, 1, 1, p)
         res_out[1] = results(1, share)
-        result_copy(1).start()
 
     pl.when(j < 2)(lambda: data_sum(wlx, dx, 0, 0, p))
 
@@ -486,15 +476,20 @@
         return carry
 
     lax.fori_loop(0, channels // slab, turn_out, 0)
+    store_ig = pltpu.make_async_copy(ig_ref, ig_hbm, stores.at[3])
+    store_cg = pltpu.make_async_copy(cg_ref, cg_hbm, stores.at[4])
+    store_ig.start()
 
     @pl.when(j < last)
     def _():
         offset = jnp.where(j == 1, share, 0)
         for f in range(2):
             cg_ref[f] = results(f, offset)
+        store_cg.start()
 
     steps[0][across]()
     steps[0][exchange]()
+    pl.when(j == 2)(lambda: result_copy(1).start())
     steps[2][gather]()
     steps[1][gather]()
     steps[0][gather]()
@@ -506,6 +501,7 @@
         for f in range(2):
             result_copy(f).wait_recv()
             cg_ref[f] = res_in[f]
+        store_cg.start()
         cache_copy().wait_send()
 
     @pl.when(j == 2)
@@ -525,7 +521,50 @@
 
     for tap in range(3):
         steps[tap][sent]()
+    store_ig.wait()
+    store_cg.wait()
     steps[0][finish]()
+
+
+def publish(scale, ig_in, cg_in, gb_in, ig_out, cg_out, wg_out, ig, cg, gb, wg, fetches, moves, reads, writes):
+    channels = ig_in.shape[0]
+    width = wg.shape[2]
+    rem = width % LANES
+    groups = LANES // rem
+    used = (width // LANES) * width + width // groups
+    read = [pltpu.make_async_copy(gb_in.at[tap], gb.at[tap], reads.at[tap]) for tap in range(3)]
+    for copy in read:
+        copy.start()
+    cut = channels // (moves.shape[0] - 2)
+    parts = [
+        (ig_in.at[n * cut:(n + 1) * cut], ig.at[n * cut:(n + 1) * cut], ig_out.at[n * cut:(n + 1) * cut])
+        for n in range(moves.shape[0] - 2)]
+    parts += [(cg_in.at[f], cg.at[f], cg_out.at[f]) for f in range(2)]
+    fetch = [pltpu.make_async_copy(src, held, fetches.at[n]) for n, (src, held, _) in enumerate(parts)]
+    move = [pltpu.make_async_copy(held, dst, moves.at[n]) for n, (_, held, dst) in enumerate(parts)]
+    for copy in fetch:
+        copy.start()
+    for copy_in, copy_out in zip(fetch, move):
+        copy_in.wait()
+        copy_out.start()
+    at = lax.broadcasted_iota(jnp.int32, (width, LANES), 1)
+    step = LANES - channels
+    write = [pltpu.make_async_copy(wg.at[tap], wg_out.at[tap], writes.at[tap]) for tap in range(3)]
+    for tap in range(3):
+        read[tap].wait()
+        first = gb[tap, :width, :].astype(F32) * scale
+        second = gb[tap, width:2 * width, :].astype(F32) * scale
+        packed = gb[tap, 2 * width:used, :].astype(F32) * scale
+        middle = jnp.where(at < step, pltpu.roll(first, step, 1), pltpu.roll(second, step, 1))
+        third = jnp.concatenate(
+            [pltpu.roll(packed, (2 * step - k * rem) % LANES, 1) if (2 * step - k * rem) % LANES else packed
+             for k in range(groups)], axis=0)
+        final = jnp.where(at < 2 * step, pltpu.roll(second, 2 * step, 1), third)
+        for b, value in enumerate((first, middle, final)):
+            wg[tap, b] = value[:, :channels]
+        write[tap].start()
+    for copy in (*move, *write):
+        copy.wait()
 
 
 def up_to(value, step):
@@ -538,20 +577,21 @@
     wide = up_to(width, LANES)
     ck = up_to(-(-(width * channels * 3) // (ns * LANES)), 16)
     scale = 1.0 / math.sqrt(nz * ns * rows * cols)
-    vmem = pl.BlockSpec(memory_space=pltpu.VMEM)
     hbm = pl.BlockSpec(memory_space=pl.ANY)
     dma = pltpu.SemaphoreType.DMA
     padded = (rows + 4) * channels
-    ig, cg, weight_grad = pl.pallas_call(
-        functools.partial(kernel, nz, ns, ck, scale),
+    ig, cg, shards = pl.pallas_call(
+        functools.partial(kernel, nz, ns, ck),
         out_shape=(
             jax.ShapeDtypeStruct(frames.shape[1:], BF16),
             jax.ShapeDtypeStruct(cache.shape, BF16),
-            jax.ShapeDtypeStruct((3, 3, width, channels), F32),
+            jax.ShapeDtypeStruct((3, ns, ck, LANES), BF16),
         ),
         in_specs=[hbm] * 4,
-        out_specs=(vmem,) * 3,
+        out_specs=(hbm,) * 3,
         scratch_shapes=[
+            pltpu.VMEM(frames.shape[1:], BF16),
+            pltpu.VMEM(cache.shape, BF16),
             pltpu.VMEM(frames.shape[1:], BF16),
             pltpu.VMEM(frames.shape[1:], BF16),
             pltpu.VMEM(cache.shape, BF16),
@@ -565,16 +605,32 @@
             pltpu.VMEM((3, ns * ck, LANES), F32),
             pltpu.VMEM((3, ns, ck, LANES), BF16), pltpu.VMEM((3, ns, ck, LANES), BF16),
             pltpu.VMEM((3, ck, LANES), BF16), pltpu.VMEM((3, nz, ck, LANES), BF16),
-            pltpu.VMEM((3, ns, ck, LANES), BF16),
+            pltpu.VMEM((3, ck, LANES), BF16),
             pltpu.VMEM(cache.shape, BF16), pltpu.VMEM(cache.shape, BF16), pltpu.VMEM(cache.shape, BF16),
             dma((4,)),
             dma((4, rows)), dma((4, rows)), dma((4, 2)), dma((4, 2)),
             dma((3, ns)), dma((3, ns)), dma((3, nz)), dma((3, nz)), dma((3, ns)), dma((3, ns)),
-            dma((2,)), dma((2, 2)),
+            dma((2,)), dma((2, 2)), dma((5,)),
         ],
         compiler_params=pltpu.CompilerParams(
             collective_id=0, has_side_effects=True, vmem_limit_bytes=60 * 1024 * 1024),
     )(grad_out[0], frames[0], cache, weight.reshape(9, width, channels))
+    ig, cg, weight_grad = pl.pallas_call(
+        functools.partial(publish, scale),
+        out_shape=(
+            jax.ShapeDtypeStruct(frames.shape[1:], BF16),
+            jax.ShapeDtypeStruct(cache.shape, BF16),
+            jax.ShapeDtypeStruct((3, 3, width, channels), F32),
+        ),
+        in_specs=[hbm] * 3,
+        out_specs=(hbm,) * 3,
+        scratch_shapes=[
+            pltpu.VMEM(frames.shape[1:], BF16), pltpu.VMEM(cache.shape, BF16),
+            pltpu.VMEM((3, ns * ck, LANES), BF16), pltpu.VMEM((3, 3, width, channels), F32),
+            dma((6,)), dma((6,)), dma((3,)), dma((3,)),
+        ],
+        compiler_params=pltpu.CompilerParams(vmem_limit_bytes=60 * 1024 * 1024),
+    )(ig, cg, shards.reshape(3, ns * ck, LANES))
     return ig[None], cg, weight_grad.reshape(weight.shape)
 
 

time: 73.2 us -> 69.2 us (0.945)
  the two profiles are of different devices: /device:TPU:25 before, /device:TPU:0 now
where the time goes in v3:
time: 69.2 us; the launch traced here: 69 us
  Pallas kernels  68.4 us (99%)
    pallas_call x1, Pallas kernels, per_device(): pl.pallas_call(functools.partial(kernel, nz, ns, ck), out_shape=(jax.Shap...  65.2 us
    pallas_call x1, Pallas kernels, per_device(): pl.pallas_call(functools.partial(publish, scale), out_shape=(jax.ShapeDty...  3.2 us

profile of v3, /device:TPU:0, one launch (start us, length us, event | category | flops | bytes accessed | tf_op | source)
XLA Modules:
  0.0 69.0 jit_solution(6055872019592930896)
XLA Ops:
  0.6 65.2 %shard_map.67 = (bf16[96,4,1280]{2,1,0:T(4,128)(2,1)}, bf16[2,24,4,1280]{3,2,1,0:T(4,128)(2,1)}, bf16[3,8,96,128]{3,2,1,0:T(8,128)(2,1)}) custom-call(bf16[96,4,1280]{2,1,0:T(4,128)(2,1)} %bitcast.6, bf16[96,4,1280]{2,1,0:T(4,128)(2,1)} %bitcast.7, bf16[2,24,4,1280]{3,2,1,0:T(4,128)(2,1)} %c_hbm.1, bf16[9,288,96]{2,1,0:T(8,128)(2,1)} %bitcast.8), custom_call_target="tpu_custom_call" | custom-call | tf_op jit(solution)/shard_map/pallas_call | solution.py:583
  65.8 3.2 %shard_map.68 = (bf16[96,4,1280]{2,1,0:T(4,128)(2,1)}, bf16[2,24,4,1280]{3,2,1,0:T(4,128)(2,1)}, f32[3,3,288,96]{3,2,1,0:T(8,128)}) custom-call(bf16[96,4,1280]{2,1,0:T(4,128)(2,1)} %get-tuple-element.9.ig_in, bf16[2,24,4,1280]{3,2,1,0:T(4,128)(2,1)} %get-tuple-element.10.cg_in, bf16[3,768,128]{2,1,0:T(8,128)(2,1)} %bitcast.9), custom_call_target="tpu_custom_call" | custom-call | tf_op jit(solution)/shard_map/pallas_call | solution.py:618

commit v4 on v3

--- a/solution.py
+++ b/solution.py
@@ -287,16 +287,20 @@
                 total = total + rb[index, lax.rem(s + ns - k, ns)].astype(F32)
             zs[index] = total.astype(BF16)
 
+        holders = nz if index == 2 else last
+
         def exchange():
+            @pl.when(j < holders)
+            def _():
+                for k in range(1, nz):
+                    z_copy(k).start()
+
+        def gather():
+            pl.when(j < holders)(lambda: zb.__setitem__((index, j), zs[index]))
             for k in range(1, nz):
-                z_copy(k).start()
-
-        def gather():
-            zb[index, j] = zs[index]
-            for k in range(1, nz):
-                z_landed(k).wait_recv()
+                pl.when(lax.rem(j + nz - k, nz) < holders)(lambda: z_landed(k).wait_recv())
             total = zb[index, 0].astype(F32)
-            for q in range(1, nz):
+            for q in range(1, holders):
                 total = total + zb[index, q].astype(F32)
             mine[index] = total.astype(BF16)
             for k in range(1, ns):
@@ -315,8 +319,10 @@
             for k in range(1, ns):
                 rs_copy(k).wait_send()
                 ag_copy(k).wait_send()
-            for k in range(1, nz):
-                z_copy(k).wait_send()
+            @pl.when(j < holders)
+            def _():
+                for k in range(1, nz):
+                    z_copy(k).wait_send()
 
         return scatter, across, exchange, gather, finish, sent
 
@@ -446,6 +452,8 @@
     final = jnp.int32(rows - 1)
     p = order[-1] + 1
     late_row(final)
+    steps[2][exchange]()
+    steps[1][exchange]()
 
     @pl.when(j < 2)
     def _():
@@ -458,8 +466,6 @@
         kernel_sum(wtc, cpad, 1, 1, p)
 
     steps[0][scatter]()
-    steps[2][exchange]()
-    steps[1][exchange]()
 
     @pl.when(j == 2)
     def _():

time: 69.2 us -> 68.4 us (0.988)
  Pallas kernels: 68.4 us -> 67.6 us
    pallas_call x1, Pallas kernels: 65.2 us -> 64.4 us  [per_device(): pl.pallas_call(functools.partial(kernel, nz, ns, ck), out_shape=(jax.Shap...]
where the time goes in v4:
time: 68.4 us; the launch traced here: 68.2 us
  Pallas kernels  67.6 us (99%)
    pallas_call x1, Pallas kernels, per_device(): pl.pallas_call(functools.partial(kernel, nz, ns, ck), out_shape=(jax.Shap...  64.4 us
    pallas_call x1, Pallas kernels, per_device(): pl.pallas_call(functools.partial(publish, scale), out_shape=(jax.ShapeDty...  3.2 us

profile of v4, /device:TPU:0, one launch (start us, length us, event | category | flops | bytes accessed | tf_op | source)
XLA Modules:
  0.0 68.2 jit_solution(9096793858588587292)
XLA Ops:
  0.6 64.4 %shard_map.67 = (bf16[96,4,1280]{2,1,0:T(4,128)(2,1)}, bf16[2,24,4,1280]{3,2,1,0:T(4,128)(2,1)}, bf16[3,8,96,128]{3,2,1,0:T(8,128)(2,1)}) custom-call(bf16[96,4,1280]{2,1,0:T(4,128)(2,1)} %bitcast.6, bf16[96,4,1280]{2,1,0:T(4,128)(2,1)} %bitcast.7, bf16[2,24,4,1280]{3,2,1,0:T(4,128)(2,1)} %c_hbm.1, bf16[9,288,96]{2,1,0:T(8,128)(2,1)} %bitcast.8), custom_call_target="tpu_custom_call" | custom-call | tf_op jit(solution)/shard_map/pallas_call | solution.py:589
  65.0 3.2 %shard_map.68 = (bf16[96,4,1280]{2,1,0:T(4,128)(2,1)}, bf16[2,24,4,1280]{3,2,1,0:T(4,128)(2,1)}, f32[3,3,288,96]{3,2,1,0:T(8,128)}) custom-call(bf16[96,4,1280]{2,1,0:T(4,128)(2,1)} %get-tuple-element.9.ig_in, bf16[2,24,4,1280]{3,2,1,0:T(4,128)(2,1)} %get-tuple-element.10.cg_in, bf16[3,768,128]{2,1,0:T(8,128)(2,1)} %bitcast.9), custom_call_target="tpu_custom_call" | custom-call | tf_op jit(solution)/shard_map/pallas_call | solution.py:624

commit v5 on v4

--- a/solution.py
+++ b/solution.py
@@ -277,7 +277,7 @@
             pack(index)
             for q in range(ns):
                 sb[index, q] = flat[index, q * ck:(q + 1) * ck, :].astype(BF16)
-            for k in range(1, ns):
+            for k in sorted(range(1, ns), key=lambda k: abs(k - ns // 2)):
                 rs_copy(k).start()
 
         def across():
@@ -303,7 +303,7 @@
             for q in range(1, holders):
                 total = total + zb[index, q].astype(F32)
             mine[index] = total.astype(BF16)
-            for k in range(1, ns):
+            for k in sorted(range(1, ns), key=lambda k: abs(k - ns // 2)):
                 ag_copy(k).start()
             keep().start()
 
@@ -318,16 +318,75 @@
         def sent():
             for k in range(1, ns):
                 rs_copy(k).wait_send()
+            if index:
+                return
+            for k in range(1, ns):
                 ag_copy(k).wait_send()
+
             @pl.when(j < holders)
             def _():
                 for k in range(1, nz):
                     z_copy(k).wait_send()
 
-        return scatter, across, exchange, gather, finish, sent
+        return scatter, across, exchange, gather, finish, sent, z_copy, z_landed
 
     steps = [reduction(tap) for tap in range(3)]
-    scatter, across, exchange, gather, finish, sent = range(6)
+    scatter, across, exchange, gather, finish, sent, z_copy, z_landed = range(8)
+
+    early = pl.ds(1, 2)
+
+    def pair_z(source, to, k):
+        return pltpu.make_async_remote_copy(
+            src_ref=zs.at[early], dst_ref=zb.at[early, source],
+            send_sem=zz_send.at[1, k], recv_sem=zz_recv.at[1, source],
+            device_id={"tm": to}, device_id_type=MESH)
+
+    def pair_ag(source, to, k):
+        return pltpu.make_async_remote_copy(
+            src_ref=mine.at[early], dst_ref=gb.at[early, source],
+            send_sem=ag_send.at[1, k], recv_sem=ag_recv.at[1, source],
+            device_id={"space": to}, device_id_type=MESH)
+
+    def pair_keep():
+        return pltpu.make_async_copy(mine.at[early], gb.at[early, s], stores.at[1])
+
+    def pair_exchange():
+        for k in range(1, nz):
+            pl.when(j < last)(lambda: pair_z(j, lax.rem(j + k, nz), k).start())
+            pl.when(j == last)(lambda: steps[2][z_copy](k).start())
+
+    def pair_gather():
+        zb[2, j] = zs[2]
+
+        @pl.when(j < last)
+        def _():
+            zb[1, j] = zs[1]
+
+        for k in range(1, nz):
+            source = lax.rem(j + nz - k, nz)
+            pl.when(source < last)(lambda: pair_z(source, source, k).wait_recv())
+            pl.when(source == last)(lambda: steps[2][z_landed](k).wait_recv())
+        for tap, holders in ((2, nz), (1, last)):
+            total = zb[tap, 0].astype(F32)
+            for q in range(1, holders):
+                total = total + zb[tap, q].astype(F32)
+            mine[tap] = total.astype(BF16)
+        for k in sorted(range(1, ns), key=lambda k: abs(k - ns // 2)):
+            pair_ag(s, lax.rem(s + k, ns), k).start()
+        pair_keep().start()
+
+    def pair_finish():
+        for k in range(1, ns):
+            source = lax.rem(s + ns - k, ns)
+            pair_ag(source, source, k).wait_recv()
+        pair_keep().wait()
+
+    def pair_sent():
+        for k in range(1, ns):
+            pair_ag(s, lax.rem(s + k, ns), k).wait_send()
+        for k in range(1, nz):
+            pl.when(j < last)(lambda: pair_z(j, lax.rem(j + k, nz), k).wait_send())
+            pl.when(j == last)(lambda: steps[2][z_copy](k).wait_send())
 
     def middle_row(e):
         r = ordered(e)
@@ -452,8 +511,7 @@
     final = jnp.int32(rows - 1)
     p = order[-1] + 1
     late_row(final)
-    steps[2][exchange]()
-    steps[1][exchange]()
+    pair_exchange()
 
     @pl.when(j < 2)
     def _():
@@ -496,11 +554,9 @@
     steps[0][across]()
     steps[0][exchange]()
     pl.when(j == 2)(lambda: result_copy(1).start())
-    steps[2][gather]()
-    steps[1][gather]()
+    pair_gather()
     steps[0][gather]()
-    steps[2][finish]()
-    steps[1][finish]()
+    pair_finish()
 
     @pl.when(j == last)
     def _():
@@ -527,6 +583,7 @@
 
     for tap in range(3):
         steps[tap][sent]()
+    pair_sent()
     store_ig.wait()
     store_cg.wait()
     steps[0][finish]()
@@ -633,7 +690,7 @@
         scratch_shapes=[
             pltpu.VMEM(frames.shape[1:], BF16), pltpu.VMEM(cache.shape, BF16),
             pltpu.VMEM((3, ns * ck, LANES), BF16), pltpu.VMEM((3, 3, width, channels), F32),
-            dma((6,)), dma((6,)), dma((3,)), dma((3,)),
+            dma((3,)), dma((3,)), dma((3,)), dma((3,)),
         ],
         compiler_params=pltpu.CompilerParams(vmem_limit_bytes=60 * 1024 * 1024),
     )(ig, cg, shards.reshape(3, ns * ck, LANES))

time: 68.4 us -> 68.3 us (level)
  no operation moved by 1% of the time
where the time goes in v5:
time: 68.3 us; the launch traced here: 68.2 us
  Pallas kernels  67.5 us (99%)
    pallas_call x1, Pallas kernels, per_device(): pl.pallas_call(functools.partial(kernel, nz, ns, ck), out_shape=(jax.Shap...  64.5 us
    pallas_call x1, Pallas kernels, per_device(): pl.pallas_call(functools.partial(publish, scale), out_shape=(jax.ShapeDty...  3.05 us

profile of v5, /device:TPU:0, one launch (start us, length us, event | category | flops | bytes accessed | tf_op | source)
XLA Modules:
  0.0 68.2 jit_solution(4123543288944112654)
XLA Ops:
  0.6 64.5 %shard_map.67 = (bf16[96,4,1280]{2,1,0:T(4,128)(2,1)}, bf16[2,24,4,1280]{3,2,1,0:T(4,128)(2,1)}, bf16[3,8,96,128]{3,2,1,0:T(8,128)(2,1)}) custom-call(bf16[96,4,1280]{2,1,0:T(4,128)(2,1)} %bitcast.6, bf16[96,4,1280]{2,1,0:T(4,128)(2,1)} %bitcast.7, bf16[2,24,4,1280]{3,2,1,0:T(4,128)(2,1)} %c_hbm.1, bf16[9,288,96]{2,1,0:T(8,128)(2,1)} %bitcast.8), custom_call_target="tpu_custom_call" | custom-call | tf_op jit(solution)/shard_map/pallas_call | solution.py:646
  65.1 3.0 %shard_map.68 = (bf16[96,4,1280]{2,1,0:T(4,128)(2,1)}, bf16[2,24,4,1280]{3,2,1,0:T(4,128)(2,1)}, f32[3,3,288,96]{3,2,1,0:T(8,128)}) custom-call(bf16[96,4,1280]{2,1,0:T(4,128)(2,1)} %get-tuple-element.9.ig_in, bf16[2,24,4,1280]{3,2,1,0:T(4,128)(2,1)} %get-tuple-element.10.cg_in, bf16[3,768,128]{2,1,0:T(8,128)(2,1)} %bitcast.9), custom_call_target="tpu_custom_call" | custom-call | tf_op jit(solution)/shard_map/pallas_call | solution.py:681
